TPU v7x, 256 devices: a whole 4x4x8 slice. The times are simulated.
256 devices in a mesh: section: 4 (over z_hi, core), dp: 64 (over z_lo, y, x).
Axes of the slice: x: 4, y: 4, z: 8 (z_hi: 2, z_lo: 4; z = z_hi * 4 + z_lo), core: 2. Of those that a mesh axis runs over, the one named last changes fastest.
Arguments:
- layer_inputs: bfloat16 [4, 64, 512, 4096], P('section', 'dp'), may hold values from -6 to 6
- out_grads: bfloat16 [4, 64, 512, 4096], P('section', 'dp'), may hold values from -6 to 6
- projections: bfloat16 [4, 4096, 128], P('section'), may hold values from -0.09375 to 0.09375
- query_grads: bfloat16 [4, 2048, 4096], P('section', 'dp'), may hold values from -0.59765625 to 0.59765625
- lengths: int32 [64], P('dp'), may hold values from 1 to 512, as said below
Outputs:
- scores: float32 [64, 2048], P('dp', 'section')
Inputs may be any that keep to these rules, and one draw needn't show every extreme that they name: `lengths`: some training example fills all 512 slots.
All inputs are finite; a program needn't handle non-finite values.
Results may differ from a plain program's by a relative error of at most 0.005.
Values may be sent and summed in bfloat16 or wider, within the bound.
No kernel may reach another device: no remote copies, remote signals or barrier semaphores. Data moves between devices by JAX's collectives and lax.ppermute only.
A program may use at most 128 MiB of HBM per device.

v0:
```python
import jax
import jax.numpy as jnp
from jax import lax
from jax.sharding import PartitionSpec as P


def project_layer(inputs, grads, proj_table, valid_mask, token_count):
    low_rank = proj_table.shape[1] // 2
    ex_rows, seq_len, model_width = inputs.shape
    input_side = jnp.dot(
        inputs.reshape(ex_rows * seq_len, model_width),
        proj_table[:, :low_rank],
        preferred_element_type=jnp.float32,
    )
    input_side = input_side.astype(jnp.bfloat16).reshape(ex_rows, seq_len, low_rank)
    grad_side = jnp.dot(
        grads.reshape(ex_rows * seq_len, model_width),
        proj_table[:, low_rank:],
        preferred_element_type=jnp.float32,
    )
    grad_side = grad_side.astype(jnp.bfloat16).reshape(ex_rows, seq_len, low_rank)
    masked = grad_side * valid_mask[:, :, None]
    summed = (
        jnp.einsum("esa,esb->eab", masked, input_side, preferred_element_type=jnp.float32)
        / token_count[:, None, None]
    )
    return summed.astype(jnp.bfloat16).reshape(ex_rows, low_rank * low_rank)


def on_device(layer_inputs, out_grads, projections, query_grads, lengths):
    seq_len = layer_inputs.shape[2]
    valid_mask = (
        lax.broadcasted_iota(jnp.int32, (lengths.shape[0], seq_len), 1) < lengths[:, None]
    ).astype(jnp.bfloat16)
    token_count = lengths.astype(jnp.float32)
    example_grads = jnp.stack(
        [project_layer(layer_inputs[0], out_grads[0], projections[0], valid_mask, token_count)]
    )
    score_block = jnp.einsum(
        "ler,lqr->eq",
        lax.all_gather(example_grads, "dp", axis=1, tiled=True),
        query_grads,
        preferred_element_type=jnp.float32,
    )
    partial_value = lax.all_to_all(score_block, "dp", split_axis=0, concat_axis=1, tiled=True)
    return lax.psum_scatter(partial_value, "section", scatter_dimension=1, tiled=True)


def solution(mesh):
    placed = (
        P("section", "dp", None, None),
        P("section", "dp", None, None),
        P("section", None, None),
        P("section", "dp", None),
        P("dp"),
    )
    return jax.shard_map(
        on_device, mesh=mesh, in_specs=placed, out_specs=P("dp", "section"), check_vma=False
    )
```

profile of v0, /device:TPU:1, one launch (start us, length us, event | category | flops | bytes accessed | tf_op | source)
XLA Modules:
  0.0 278.2 jit_solution(2024502826622382864)
XLA Ops:
  6.5 0.0 copy-start
  6.5 0.0 copy-start.1
  6.5 0.0 reduce-scatter.4.cloned.1.call-start
  7.3 4.2 %fusion.13 = bf16[512,64]{0,1:T(8,128)(2,1)S(1)} fusion(bf16[1,1,512,4096]{3,2,1,0:T(8,128)(2,1)} %param.6, bf16[4096,128]{1,0:T(8,128)(2,1)} %bitcast.34, bf16[512]{0:T(512)(128)(2,1)S(1)} %fusion.29), kind=kOutput, calls=%fused_computation.7 | convolution fusion | flops 268500992 | bytes 5309440 | tf_op jit(solution)/shard_map/dot_general | solution.py:16
  11.5 0.0 copy-done.1
  11.5 3.7 %fusion.19 = bf16[64,64]{1,0:T(8,128)(2,1)S(1)} fusion(bf16[512,64]{0,1:T(8,128)(2,1)S(1)} %fusion.13, bf16[1,1,512,4096]{3,2,1,0:T(8,128)(2,1)} %param.5, bf16[4096,128]{1,0:T(8,128)(2,1)S(1)} %bitcast.35, f32[]{:T(128)} %bitcast.4), kind=kOutput, calls=%fused_computation.9 | convolution fusion | flops 272670720 | bytes 5316612 | tf_op jit(solution)/shard_map/esa,esb->eab/dot_general | solution.py:24
  15.3 0.1 stack_reshape.3
  15.3 166.6 %all_gather.3 = bf16[1,64,4096]{2,0,1:T(2,128)(2,1)S(1)} all-gather(bf16[1,1,4096]{2,0,1:T(2,128)(2,1)S(1)} %bitcast.38), channel_id=1, replica_groups=mesh['section'=4,'dp'=64] {'dp'}, dimensions={1}, use_global_device_ids=true | all-gather | bytes 532480 | tf_op jit(solution)/shard_map/all_gather | solution.py:41
  181.9 0.0 copy-done
  181.9 0.7 fusion.25
  182.6 12.8 %all_to_all.17 = f32[64,1,32]{2,1,0:T(1,128)S(1)} all-to-all(f32[64,1,32]{2,1,0:T(1,128)S(1)} %bitcast.39), channel_id=1, replica_groups=mesh['section'=4,'dp'=64] {'dp'}, dimensions={0} | all-to-all | bytes 16384 | tf_op jit(solution)/shard_map/all_to_all | solution.py:45
  195.4 0.5 broadcast.14
  195.9 0.7 reduce.3
  196.7 2.1 all_to_all.15
  198.7 0.0 reduce-scatter.4.cloned.1.call-update
  198.8 71.0 %reduce-scatter.4.cloned.1.call-done = f32[512,1]{1,0:T(8,128)} async-done(((f32[2048,1]{1,0:T(8,128)}), f32[512,1]{1,0:T(8,128)}) %reduce-scatter.4.cloned.1.call-update) | async-done | bytes 2064
  269.7 1.6 copy.12
  (1 shorter events, 0.0 us)
Async XLA Ops:
  6.5 175.4 %copy-start = (bf16[1,32,4096]{2,1,0:T(8,128)(2,1)S(1)}, bf16[1,32,4096]{2,1,0:T(8,128)(2,1)}, u32[]{:S(2)}) copy-start(bf16[1,32,4096]{2,1,0:T(8,128)(2,1)} %param.8) | copy-start | bytes 786436
  6.5 5.0 %copy-start.1 = (bf16[1,4096,128]{2,1,0:T(8,128)(2,1)S(1)}, bf16[1,4096,128]{2,1,0:T(8,128)(2,1)}, u32[]{:S(2)}) copy-start(bf16[1,4096,128]{2,1,0:T(8,128)(2,1)} %param.7) | copy-start | bytes 3145732
  6.5 263.2 %reduce-scatter.4.cloned.1.call-start = ((), (), s32[]{:S(2)}) async-start(), calls=%async_computation.2 | async-start | bytes 1310720
Sparse Core Ops, SparseCore 0:
  198.9 70.7 reduce-scatter.3
where the time goes:
time: 278 us
  blocking collectives  179 us (64%)
  waiting for transfers between devices  71 us (26%)
  between operations  14.2 us (5%)
  matrix products  8.61 us (3%)
  local copies, waits for them, and re-layouts  4.32 us (2%)
    all_gather x1, blocking collectives, on_device(): lax.all_gather(example_grads, 'dp', axis=1, tiled=True)  167 us
    unnamed x2, waiting for transfers between devices  71 us
    all_to_all x1, blocking collectives, on_device(): lax.all_to_all(score_block, 'dp', split_axis=0, concat_axis=1, tiled=True)  12.8 us
  transfers between devices with their start and end apart: 1, of which 1 were waited for; matrix products, arithmetic and copies ran while one was open for 0% of the time, Pallas kernels for 0%

commit v1 on v0

--- a/solution.py
+++ b/solution.py
@@ -38,7 +38,9 @@
     )
     score_block = jnp.einsum(
         "ler,lqr->eq",
-        lax.all_gather(example_grads, "dp", axis=1, tiled=True),
+        jnp.concatenate(
+            lax.all_to_all(jnp.stack([example_grads] * lax.axis_size("dp")), "dp", 0, 0), axis=1
+        ),
         query_grads,
         preferred_element_type=jnp.float32,
     )

time: 278 us -> 122 us (0.44)
  blocking collectives: 179 us -> 43.3 us
  waiting for transfers between devices: 71 us -> 43.9 us
  other arithmetic: 0.73 us -> 4.52 us
    all_gather x1 -> x0, blocking collectives: 167 us -> none  [on_device(): lax.all_gather(example_grads, 'dp', axis=1, tiled=True)]
    all_to_all x0 -> x1, blocking collectives: none -> 29.3 us  [on_device(): lax.all_to_all(jnp.stack([example_grads] * lax.axis_size('dp')), 'dp', 0, 0)]
    unnamed x2, waiting for transfers between devices: 71 us -> 43.9 us
    another operation x0 -> x1, other arithmetic: none -> 3.79 us  [on_device(): jnp.stack([example_grads] * lax.axis_size('dp'))]
where the time goes in v1:
time: 122 us; the launch traced here: 121 us
  waiting for transfers between devices  43.9 us (36%)
  blocking collectives  43.3 us (35%)
  between operations  14.2 us (12%)
  matrix products  8.6 us (7%)
  local copies, waits for them, and re-layouts  6.75 us (6%)
  other arithmetic  4.52 us (4%)
    unnamed x2, waiting for transfers between devices  43.9 us
    all_to_all x1, blocking collectives, on_device(): lax.all_to_all(jnp.stack([example_grads] * lax.axis_size('dp')), 'dp', 0, 0)  29.3 us
    all_to_all x1, blocking collectives, on_device(): lax.all_to_all(score_block, 'dp', split_axis=0, concat_axis=1, tiled=True)  14 us
    dot_general x1, matrix products, project_layer(): jnp.dot(grads.reshape(ex_rows * seq_len, model_width), proj_table[:, low_...  4.21 us
    another operation x1, other arithmetic, on_device(): jnp.stack([example_grads] * lax.axis_size('dp'))  3.79 us
    dot_general x1, matrix products, project_layer(): jnp.einsum('esa,esb->eab', masked, input_side, preferred_element_type=jnp...  3.72 us
    all_to_all x2, local copies, waits for them, and re-layouts, on_device(): lax.all_to_all(score_block, 'dp', split_axis=0, concat_axis=1, tiled=True)  2.58 us
    unnamed x7, local copies, waits for them, and re-layouts  2.55 us
  transfers between devices with their start and end apart: 1, of which 1 were waited for; matrix products, arithmetic and copies ran while one was open for 0% of the time, Pallas kernels for 0%

profile of v1, /device:TPU:1, one launch (start us, length us, event | category | flops | bytes accessed | tf_op | source)
XLA Modules:
  0.0 121.3 jit_solution(3420363889700070760)
XLA Ops:
  6.5 0.0 copy-start
  6.5 0.0 copy-start.1
  6.5 0.0 reduce-scatter.4.cloned.1.call-start
  7.3 4.2 %fusion.13 = bf16[512,64]{0,1:T(8,128)(2,1)S(1)} fusion(bf16[1,1,512,4096]{3,2,1,0:T(8,128)(2,1)} %param.6, bf16[4096,128]{1,0:T(8,128)(2,1)} %bitcast.33, bf16[512]{0:T(512)(128)(2,1)S(1)} %fusion.29), kind=kOutput, calls=%fused_computation.7 | convolution fusion | flops 268500992 | bytes 5309440 | tf_op jit(solution)/shard_map/dot_general | solution.py:16
  11.5 0.0 copy-done.1
  11.5 3.7 %fusion.19 = bf16[64,64]{1,0:T(8,128)(2,1)S(1)} fusion(bf16[512,64]{0,1:T(8,128)(2,1)S(1)} %fusion.13, bf16[1,1,512,4096]{3,2,1,0:T(8,128)(2,1)} %param.5, bf16[4096,128]{1,0:T(8,128)(2,1)S(1)} %bitcast.34, f32[]{:T(128)} %bitcast.4), kind=kOutput, calls=%fused_computation.9 | convolution fusion | flops 272670720 | bytes 5316612 | tf_op jit(solution)/shard_map/esa,esb->eab/dot_general | solution.py:24
  15.3 0.1 stack_stack_reshape.2
  15.3 1.0 stack.3
  16.4 0.5 broadcast.17
  16.9 3.8 %reduce.4 = bf16[64,4096]{1,0:T(8,128)(2,1)S(1)} reduce(bf16[64,1,1,4096]{3,2,1,0:T(2,128)(2,1)S(1)} %stack.3, bf16[]{:T(256)} %broadcast.17), dimensions={1,2}, to_apply=%stack.3.reduce_sub_computation | reduce | bytes 1048578 | tf_op jit(solution)/shard_map/stack | solution.py:42
  20.7 0.4 reshape.58
  21.1 29.3 %all_to_all.22 = bf16[64,2,2048]{2,1,0:T(2,128)(2,1)S(1)} all-to-all(bf16[64,2,2048]{2,1,0:T(2,128)(2,1)S(1)} %reshape.58), channel_id=1, replica_groups=mesh['section'=4,'dp'=64] {'dp'}, dimensions={0} | all-to-all | bytes 1048576 | tf_op jit(solution)/shard_map/all_to_all | solution.py:42
  50.3 0.5 reshape.59
  50.8 0.0 copy-done
  50.9 0.7 fusion.25
  51.5 14.0 %all_to_all.23 = f32[64,1,32]{2,1,0:T(1,128)S(1)} all-to-all(f32[64,1,32]{2,1,0:T(1,128)S(1)} %bitcast.37), channel_id=1, replica_groups=mesh['section'=4,'dp'=64] {'dp'}, dimensions={0} | all-to-all | bytes 16384 | tf_op jit(solution)/shard_map/all_to_all | solution.py:47
  65.6 0.5 broadcast.16
  66.1 0.7 reduce.3
  66.8 2.1 %all_to_all.19 = f32[1,2048]{0,1:T(8,128)} reshape(f32[64,32]{1,0:T(8,128)S(1)} %reduce.3) | data formatting | bytes 16384 | tf_op jit(solution)/shard_map/all_to_all | solution.py:47
  68.9 0.0 reduce-scatter.4.cloned.1.call-update
  68.9 43.9 %reduce-scatter.4.cloned.1.call-done = f32[512,1]{1,0:T(8,128)} async-done(((f32[2048,1]{1,0:T(8,128)}), f32[512,1]{1,0:T(8,128)}) %reduce-scatter.4.cloned.1.call-update) | async-done | bytes 2064
  112.8 1.6 %copy.9 = f32[1,512]{1,0:T(1,128)} copy(f32[1,512]{0,1:T(8,128)} %bitcast.36) | data formatting | bytes 4096
  (1 shorter events, 0.0 us)
Async XLA Ops:
  6.5 44.3 %copy-start = (bf16[1,32,4096]{2,1,0:T(8,128)(2,1)S(1)}, bf16[1,32,4096]{2,1,0:T(8,128)(2,1)}, u32[]{:S(2)}) copy-start(bf16[1,32,4096]{2,1,0:T(8,128)(2,1)} %param.8) | copy-start | bytes 786436
  6.5 5.0 %copy-start.1 = (bf16[1,4096,128]{2,1,0:T(8,128)(2,1)S(1)}, bf16[1,4096,128]{2,1,0:T(8,128)(2,1)}, u32[]{:S(2)}) copy-start(bf16[1,4096,128]{2,1,0:T(8,128)(2,1)} %param.7) | copy-start | bytes 3145732
  6.5 106.3 %reduce-scatter.4.cloned.1.call-start = ((), (), s32[]{:S(2)}) async-start(), calls=%async_computation.3 | async-start | bytes 1310720
Sparse Core Ops, SparseCore 0:
  69.0 43.7 reduce-scatter.3
